TPU v7x, 512 devices: a whole 4x8x8 slice. The times are simulated.
512 devices in a mesh: dp: 16 (over z, core), mp: 32 (over y, x).
Axes of the slice: x: 4, y: 8, z: 8, core: 2. Of those that a mesh axis runs over, the one named last changes fastest.
Arguments:
- inputs: bfloat16 [32768, 4096], P('dp', 'mp'), may hold values from -6 to 6
- out_grad: bfloat16 [32768, 4096], P('dp', 'mp'), may hold values from -6 to 6
- mean_state: float32 [6, 64, 64, 64], P(None, 'mp', 'dp'), may hold values from -0.75 to 0.75
- hess_state: float32 [6, 64, 64, 64], P(None, 'mp', 'dp'), may hold values from 2 to 20
- grad_state: float32 [6, 64, 64, 64], P(None, 'mp', 'dp'), may hold values from -1.8 to 1.8
- noise_draw: float32 [16, 6, 64, 64, 64], P('dp', None, 'mp'), may hold values from -6 to 6
Outputs:
- new_mean: float32 [6, 64, 64, 64], P(None, 'mp', 'dp')
- new_hess: float32 [6, 64, 64, 64], P(None, 'mp', 'dp')
- new_grad: float32 [6, 64, 64, 64], P(None, 'mp', 'dp')
All inputs are finite; a program needn't handle non-finite values.
Results may differ from a plain program's by a relative error of at most 0.0018.
Values may be sent and summed in bfloat16 or wider, within the bound.
No kernel may reach another device: no remote copies, remote signals or barrier semaphores. Data moves between devices by JAX's collectives and lax.ppermute only.
A program may use at most 64 MiB of HBM per device.

v0:
```python
import jax
import jax.numpy as jnp
from jax import lax
from jax.sharding import PartitionSpec as P

LAMBDA_SIZE = 100.0
DELTA_DAMP = 0.001
BETA_GRAD = 0.9
BETA_HESS = 0.9
STEP_RATE = 1.0


def bdot(form, left, right):
    return jnp.einsum(form, left, right, preferred_element_type=jnp.float32)


def silu_slope(value):
    sigm = jax.nn.sigmoid(value)
    return sigm * (1.0 + value * (1.0 - sigm))


def per_device(inputs, out_grad, mean_state, hess_state, grad_state, noise_draw):
    tokens = inputs.shape[0]
    local_blocks = mean_state.shape[1]
    width = mean_state.shape[3]
    scale = tokens ** (-0.5)
    full_mean, full_hess = (
        lax.all_gather(mean_state, "dp", axis=2, tiled=True),
        lax.all_gather(hess_state, "dp", axis=2, tiled=True),
    )
    spread = jnp.sqrt(LAMBDA_SIZE * (full_hess + DELTA_DAMP))
    noise = noise_draw[0]
    sampled = (full_mean + noise / spread).astype(jnp.bfloat16)
    in_rows = inputs.reshape(tokens, local_blocks, width)
    grad_rows = out_grad.reshape(tokens, local_blocks, width)
    y_left = bdot("tbr,brc->tcb", in_rows, sampled[0]).astype(jnp.bfloat16)
    y_right = bdot("tbr,brc->tcb", in_rows, sampled[2]).astype(jnp.bfloat16)
    perm_left = lax.all_to_all(y_left, "mp", split_axis=1, concat_axis=2, tiled=True)
    perm_right = lax.all_to_all(y_right, "mp", split_axis=1, concat_axis=2, tiled=True)
    u_left = bdot("tji,jic->tjc", perm_left, sampled[1])
    u_right = bdot("tji,jic->tjc", perm_right, sampled[3])
    hidden = (jax.nn.silu(u_left) * u_right).astype(jnp.bfloat16)
    outer = bdot("tbr,brc->tcb", hidden, sampled[4]).astype(jnp.bfloat16)
    perm_left, perm_right, u_left, u_right, hidden, outer = (
        perm_left,
        perm_right,
        u_left,
        u_right,
        hidden,
        outer,
    )
    mixed_rows = lax.all_to_all(outer, "mp", split_axis=1, concat_axis=2, tiled=True)
    back_outer = bdot("tjc,jic->tij", grad_rows, sampled[5]).astype(jnp.bfloat16)
    back_hidden = lax.all_to_all(back_outer, "mp", split_axis=1, concat_axis=2, tiled=True)
    grad_five = bdot("tji,tjc->jic", mixed_rows, grad_rows) * scale
    grad_four = bdot("tbr,tbc->brc", hidden, back_hidden) * scale
    d_hidden = bdot("tbc,brc->tbr", back_hidden, sampled[4])
    gate_grad = (d_hidden * u_right * silu_slope(u_left)).astype(jnp.bfloat16)
    value_grad = (d_hidden * jax.nn.silu(u_left)).astype(jnp.bfloat16)
    grad_one = bdot("tji,tjc->jic", perm_left, gate_grad) * scale
    grad_three = bdot("tji,tjc->jic", perm_right, value_grad) * scale
    back_left = bdot("tjc,jic->tij", gate_grad, sampled[1]).astype(jnp.bfloat16)
    back_right = bdot("tjc,jic->tij", value_grad, sampled[3]).astype(jnp.bfloat16)
    rows_left, rows_right = (
        lax.all_to_all(back_left, "mp", split_axis=1, concat_axis=2, tiled=True),
        lax.all_to_all(back_right, "mp", split_axis=1, concat_axis=2, tiled=True),
    )
    grad_zero = bdot("tbr,tbc->brc", in_rows, rows_left) * scale
    grad_two = bdot("tbr,tbc->brc", in_rows, rows_right) * scale
    all_grads = jnp.stack([grad_zero, grad_one, grad_two, grad_three, grad_four, grad_five])
    grad_sum, hess_sum = (
        lax.psum_scatter(all_grads, "dp", scatter_dimension=2, tiled=True),
        lax.psum_scatter(all_grads * noise * spread, "dp", scatter_dimension=2, tiled=True),
    )
    groups = lax.axis_size("dp")
    grad_avg = grad_sum / groups
    hess_avg = hess_sum / groups
    new_grad = BETA_GRAD * grad_state + (1.0 - BETA_GRAD) * grad_avg
    new_hess = (
        BETA_HESS * hess_state
        + (1.0 - BETA_HESS) * hess_avg
        + 0.5 * (1.0 - BETA_HESS) ** 2 * (hess_state - hess_avg) ** 2 / (hess_state + DELTA_DAMP)
    )
    new_mean = mean_state - STEP_RATE * (new_grad + DELTA_DAMP * mean_state) / (
        new_hess + DELTA_DAMP
    )
    return (new_mean, new_hess, new_grad)


def solution(mesh):
    return jax.shard_map(
        per_device,
        mesh=mesh,
        in_specs=(
            P("dp", "mp"),
            P("dp", "mp"),
            P(None, "mp", "dp", None),
            P(None, "mp", "dp", None),
            P(None, "mp", "dp", None),
            P("dp", None, "mp", None, None),
        ),
        out_specs=(P(None, "mp", "dp", None), P(None, "mp", "dp", None), P(None, "mp", "dp", None)),
        check_vma=False,
    )
```

profile of v0, /device:TPU:1, one launch (start us, length us, event | category | flops | bytes accessed | tf_op | source)
XLA Modules:
  0.0 319.1 jit_solution(12250809010809188880)
XLA Ops:
  7.2 0.8 copy.44
  8.0 25.6 %all_gather.7 = f32[6,2,64,64]{3,1,0,2:T(2,128)S(1)} all-gather(f32[6,2,4,64]{3,1,0,2:T(2,128)S(1)} %copy.44), channel_id=1, replica_groups=mesh['dp'=16,'mp'=32] {'dp'}, dimensions={2}, use_global_device_ids=true | all-gather | bytes 208896 | tf_op jit(solution)/shard_map/all_gather | solution.py:29
  33.5 0.8 copy.43
  34.3 15.5 %all_gather.6 = f32[6,2,64,64]{3,1,0,2:T(2,128)S(1)} all-gather(f32[6,2,4,64]{3,1,0,2:T(2,128)S(1)} %copy.43), channel_id=1, replica_groups=mesh['dp'=16,'mp'=32] {'dp'}, dimensions={2}, use_global_device_ids=true | all-gather | bytes 208896 | tf_op jit(solution)/shard_map/all_gather | solution.py:28
  49.8 0.2 copy.50
  50.1 0.8 copy-done.2
  50.8 0.2 fusion.18
  51.0 0.3 fusion.2
  51.4 1.4 copy.56
  52.7 9.8 %all-to-all-start.2 = ((bf16[2048,64,2]{0,2,1:T(2,128)(2,1)}), bf16[2048,64,2]{0,2,1:T(2,128)(2,1)S(1)}, u32[]{:S(2)}, u32[]{:S(2)}) async-start(bf16[2048,64,2]{0,2,1:T(2,128)(2,1)} %copy.56), calls=%async_computation.2 | async-start | bytes 1048576 | tf_op jit(solution)/shard_map/all_to_all | solution.py:38
  62.6 0.2 copy.47
  62.8 0.3 fusion
  63.1 1.4 copy.48
  64.4 14.8 %all-to-all-done.2 = bf16[2048,64,2]{0,2,1:T(2,128)(2,1)S(1)} async-done(((bf16[2048,64,2]{0,2,1:T(2,128)(2,1)}), bf16[2048,64,2]{0,2,1:T(2,128)(2,1)S(1)}, u32[]{:S(2)}, u32[]{:S(2)}) %all-to-all-start.2) | async-done | bytes 524320 | tf_op jit(solution)/shard_map/all_to_all | solution.py:38
  79.2 5.1 %all-to-all-start = ((bf16[2048,64,2]{0,2,1:T(2,128)(2,1)}), bf16[2048,64,2]{0,2,1:T(2,128)(2,1)S(1)}, u32[]{:S(2)}, u32[]{:S(2)}) async-start(bf16[2048,64,2]{0,2,1:T(2,128)(2,1)} %copy.48), calls=%async_computation | async-start | bytes 1048576 | tf_op jit(solution)/shard_map/all_to_all | solution.py:54
  84.3 0.3 fusion.1
  84.7 1.3 copy.52
  86.0 13.7 %all-to-all-done = bf16[2048,64,2]{0,2,1:T(2,128)(2,1)S(1)} async-done(((bf16[2048,64,2]{0,2,1:T(2,128)(2,1)}), bf16[2048,64,2]{0,2,1:T(2,128)(2,1)S(1)}, u32[]{:S(2)}, u32[]{:S(2)}) %all-to-all-start) | async-done | bytes 524320 | tf_op jit(solution)/shard_map/all_to_all | solution.py:54
  99.8 6.1 %all-to-all-start.1 = ((bf16[2048,64,2]{0,2,1:T(2,128)(2,1)}), bf16[2048,64,2]{0,2,1:T(2,128)(2,1)S(1)}, u32[]{:S(2)}, u32[]{:S(2)}) async-start(bf16[2048,64,2]{0,2,1:T(2,128)(2,1)} %copy.52), calls=%async_computation.1 | async-start | bytes 1048576 | tf_op jit(solution)/shard_map/all_to_all | solution.py:39
  105.9 0.4 copy.96
  106.2 0.2 all_to_all.89
  106.4 0.4 copy.98
  106.8 0.2 all_to_all.81
  107.0 2.1 convolution_bitcast_fusion
  109.1 2.0 convolution_bitcast_fusion.2
  111.1 10.0 %all-to-all-done.1 = bf16[2048,64,2]{0,2,1:T(2,128)(2,1)S(1)} async-done(((bf16[2048,64,2]{0,2,1:T(2,128)(2,1)}), bf16[2048,64,2]{0,2,1:T(2,128)(2,1)S(1)}, u32[]{:S(2)}, u32[]{:S(2)}) %all-to-all-start.1) | async-done | bytes 524320 | tf_op jit(solution)/shard_map/all_to_all | solution.py:39
  121.1 0.4 copy.97
  121.5 0.2 all_to_all.85
  121.7 3.1 multiply_convert_fusion
  124.7 1.0 fusion.3
  125.8 1.4 copy.59
  127.1 6.4 %all-to-all-start.3 = ((bf16[2048,64,2]{0,2,1:T(2,128)(2,1)}), bf16[2048,64,2]{0,2,1:T(2,128)(2,1)}, u32[]{:S(2)}, u32[]{:S(2)}) async-start(bf16[2048,64,2]{0,2,1:T(2,128)(2,1)} %copy.59), calls=%async_computation.3 | async-start | bytes 1048576 | tf_op jit(solution)/shard_map/all_to_all | solution.py:65
  133.6 1.3 fusion.4
  134.9 1.3 copy.61
  136.2 12.5 %all-to-all-done.3 = bf16[2048,64,2]{0,2,1:T(2,128)(2,1)} async-done(((bf16[2048,64,2]{0,2,1:T(2,128)(2,1)}), bf16[2048,64,2]{0,2,1:T(2,128)(2,1)}, u32[]{:S(2)}, u32[]{:S(2)}) %all-to-all-start.3) | async-done | bytes 524320 | tf_op jit(solution)/shard_map/all_to_all | solution.py:65
  148.7 6.6 %all-to-all-start.4 = ((bf16[2048,64,2]{0,2,1:T(2,128)(2,1)}), bf16[2048,64,2]{0,2,1:T(2,128)(2,1)}, u32[]{:S(2)}, u32[]{:S(2)}) async-start(bf16[2048,64,2]{0,2,1:T(2,128)(2,1)} %copy.61), calls=%async_computation.4 | async-start | bytes 1048576 | tf_op jit(solution)/shard_map/all_to_all | solution.py:66
  155.4 1.1 fusion.5
  156.5 1.4 copy.64
  157.8 2.2 copy.95
  160.0 2.0 all_to_all.93
  162.1 1.9 fusion.15
  164.0 6.4 %all-to-all-done.4 = bf16[2048,64,2]{0,2,1:T(2,128)(2,1)} async-done(((bf16[2048,64,2]{0,2,1:T(2,128)(2,1)}), bf16[2048,64,2]{0,2,1:T(2,128)(2,1)}, u32[]{:S(2)}, u32[]{:S(2)}) %all-to-all-start.4) | async-done | bytes 524320 | tf_op jit(solution)/shard_map/all_to_all | solution.py:66
  170.4 6.3 %all-to-all-start.5 = ((bf16[2048,64,2]{0,2,1:T(2,128)(2,1)}), bf16[2048,64,2]{0,2,1:T(2,128)(2,1)}, u32[]{:S(2)}, u32[]{:S(2)}) async-start(bf16[2048,64,2]{0,2,1:T(2,128)(2,1)} %copy.64), calls=%async_computation.5 | async-start | bytes 1048576 | tf_op jit(solution)/shard_map/all_to_all | solution.py:52
  176.6 0.0 all-reduce.5.cloned.1.call-start
  176.7 2.2 copy.94
  178.9 2.0 all_to_all.97
  180.9 2.0 fusion.12
  182.9 0.9 copy.66
  183.9 0.7 copy.67
  184.6 0.6 constant_dynamic-update-slice_fusion.1
  185.2 2.0 fusion.14
  187.2 0.6 constant_dynamic-update-slice_fusion
  187.9 0.9 fusion.11
  188.8 0.9 fusion.9
  189.7 2.0 all-to-all-done.5
  191.7 1.4 copy.93
  193.1 0.2 all_to_all.101
  193.3 0.9 fusion.7
  194.2 0.1 copy-done.3
  194.3 1.9 fusion.19
  196.2 0.0 all-reduce.5.cloned.1.call-update
  196.2 1.3 dynamic-slice
  198.2 112.6 %all-reduce.5.cloned.1.call-done = (f32[6,2,64,64]{3,2,1,0:T(8,128)}, f32[6,2,64,64]{3,2,1,0:T(8,128)}) async-done(((f32[6,2,64,64]{3,2,1,0:T(8,128)}, f32[6,2,64,64]{3,2,1,0:T(8,128)}), (f32[6,2,64,64]{3,2,1,0:T(8,128)}, f32[6,2,64,64]{3,2,1,0:T(8,128)})) %all-reduce.5.cloned.1.call-update) | async-done | bytes 393232
  310.7 1.5 divide_subtract_fusion
  (22 shorter events, 0.0 us)
Async XLA Ops:
  7.2 42.7 %copy-start.5 = (bf16[2048,128]{1,0:T(8,128)(2,1)S(1)}, bf16[2048,128]{1,0:T(8,128)(2,1)}, u32[]{:S(2)}) copy-start(bf16[2048,128]{1,0:T(8,128)(2,1)} %param.6) | copy-start | bytes 1572868
  49.8 1.0 copy-start.2
  51.0 33.3 %copy-start.4 = (bf16[6,2,64,64]{3,2,1,0:T(8,128)(2,1)}, bf16[6,2,64,64]{3,2,1,0:T(8,128)(2,1)S(1)}, u32[]{:S(2)}) copy-start(bf16[6,2,64,64]{3,2,1,0:T(8,128)(2,1)S(1)} %fusion.18) | copy-start | bytes 294916
  52.7 9.8 %copy-start.6 = (bf16[2048,128]{1,0:T(8,128)(2,1)S(1)}, bf16[2048,128]{1,0:T(8,128)(2,1)}, u32[]{:S(2)}) copy-start(bf16[2048,128]{1,0:T(8,128)(2,1)} %param.7) | copy-start | bytes 1572868
  52.7 26.5 %all-to-all-start.2 = ((bf16[2048,64,2]{0,2,1:T(2,128)(2,1)}), bf16[2048,64,2]{0,2,1:T(2,128)(2,1)S(1)}, u32[]{:S(2)}, u32[]{:S(2)}) async-start(bf16[2048,64,2]{0,2,1:T(2,128)(2,1)} %copy.56), calls=%async_computation.2 | async-start | bytes 1048576 | tf_op jit(solution)/shard_map/all_to_all | solution.py:38
  79.2 20.5 %all-to-all-start = ((bf16[2048,64,2]{0,2,1:T(2,128)(2,1)}), bf16[2048,64,2]{0,2,1:T(2,128)(2,1)S(1)}, u32[]{:S(2)}, u32[]{:S(2)}) async-start(bf16[2048,64,2]{0,2,1:T(2,128)(2,1)} %copy.48), calls=%async_computation | async-start | bytes 1048576 | tf_op jit(solution)/shard_map/all_to_all | solution.py:54
  99.8 21.3 %all-to-all-start.1 = ((bf16[2048,64,2]{0,2,1:T(2,128)(2,1)}), bf16[2048,64,2]{0,2,1:T(2,128)(2,1)S(1)}, u32[]{:S(2)}, u32[]{:S(2)}) async-start(bf16[2048,64,2]{0,2,1:T(2,128)(2,1)} %copy.52), calls=%async_computation.1 | async-start | bytes 1048576 | tf_op jit(solution)/shard_map/all_to_all | solution.py:39
  124.7 1.0 copy-start.1
  127.1 21.6 %all-to-all-start.3 = ((bf16[2048,64,2]{0,2,1:T(2,128)(2,1)}), bf16[2048,64,2]{0,2,1:T(2,128)(2,1)}, u32[]{:S(2)}, u32[]{:S(2)}) async-start(bf16[2048,64,2]{0,2,1:T(2,128)(2,1)} %copy.59), calls=%async_computation.3 | async-start | bytes 1048576 | tf_op jit(solution)/shard_map/all_to_all | solution.py:65
  148.7 21.6 %all-to-all-start.4 = ((bf16[2048,64,2]{0,2,1:T(2,128)(2,1)}), bf16[2048,64,2]{0,2,1:T(2,128)(2,1)}, u32[]{:S(2)}, u32[]{:S(2)}) async-start(bf16[2048,64,2]{0,2,1:T(2,128)(2,1)} %copy.61), calls=%async_computation.4 | async-start | bytes 1048576 | tf_op jit(solution)/shard_map/all_to_all | solution.py:66
  170.4 21.3 %all-to-all-start.5 = ((bf16[2048,64,2]{0,2,1:T(2,128)(2,1)}), bf16[2048,64,2]{0,2,1:T(2,128)(2,1)}, u32[]{:S(2)}, u32[]{:S(2)}) async-start(bf16[2048,64,2]{0,2,1:T(2,128)(2,1)} %copy.64), calls=%async_computation.5 | async-start | bytes 1048576 | tf_op jit(solution)/shard_map/all_to_all | solution.py:52
  176.6 134.1 %all-reduce.5.cloned.1.call-start = ((), (), s32[]{:S(2)}) async-start(), calls=%async_computation.6 | async-start | bytes 1572864
  182.9 1.0 copy-start.7
  185.2 2.0 copy-start.8
  185.2 2.7 copy-start
  193.3 1.0 copy-start.3
  196.2 114.5 %copy-start.10 = (f32[6,2,4,64]{3,2,1,0:T(4,128)S(1)}, f32[6,2,4,64]{3,2,1,0:T(4,128)}, u32[]{:S(2)}) copy-start(f32[6,2,4,64]{3,2,1,0:T(4,128)} %param.9) | copy-start | bytes 36868
  196.2 114.5 %copy-start.11 = (f32[6,2,4,64]{3,2,1,0:T(4,128)S(1)}, f32[6,2,4,64]{3,2,1,0:T(4,128)}, u32[]{:S(2)}) copy-start(f32[6,2,4,64]{3,2,1,0:T(4,128)} %param.10) | copy-start | bytes 36868
  196.2 114.5 %copy-start.9 = (f32[6,2,4,64]{3,2,1,0:T(4,128)S(1)}, f32[6,2,4,64]{3,2,1,0:T(4,128)}, u32[]{:S(2)}) copy-start(f32[6,2,4,64]{3,2,1,0:T(4,128)} %param.8) | copy-start | bytes 36868
Sparse Core Ops, SparseCore 0:
  196.3 114.3 all-reduce.4
where the time goes:
time: 321 us; the launch traced here: 319 us
  waiting for transfers between devices  172 us (54%)
  blocking collectives  41.1 us (13%)
  starting transfers between devices  40.3 us (13%)
  local copies, waits for them, and re-layouts  27 us (8%)
  matrix products  20.2 us (6%)
  between operations  14.9 us (5%)
  other arithmetic  3.57 us (1%)
    unnamed x2, waiting for transfers between devices  113 us
    all_gather x1, blocking collectives, per_device(): lax.all_gather(hess_state, 'dp', axis=2, tiled=True)  25.6 us
    dot_general x15, matrix products, bdot(): return jnp.einsum(form, left, right, preferred_element_type=jnp.float32)  20.2 us
    all_gather x1, blocking collectives, per_device(): lax.all_gather(mean_state, 'dp', axis=2, tiled=True)  15.5 us
    all_to_all x1, waiting for transfers between devices, per_device(): lax.all_to_all(y_left, 'mp', split_axis=1, concat_axis=2, tiled=True)  14.8 us
    all_to_all x1, waiting for transfers between devices, per_device(): lax.all_to_all(back_outer, 'mp', split_axis=1, concat_axis=2, tiled=True)  13.7 us
    all_to_all x1, waiting for transfers between devices, per_device(): lax.all_to_all(back_left, 'mp', split_axis=1, concat_axis=2, tiled=True)  12.5 us
    all_to_all x1, waiting for transfers between devices, per_device(): lax.all_to_all(y_right, 'mp', split_axis=1, concat_axis=2, tiled=True)  9.96 us
  transfers between devices with their start and end apart: 7, of which 7 were waited for; matrix products, arithmetic and copies ran while one was open for 9% of the time, Pallas kernels for 0%

commit v1 on v0

--- a/solution.py
+++ b/solution.py
@@ -8,6 +8,22 @@
 BETA_GRAD = 0.9
 BETA_HESS = 0.9
 STEP_RATE = 1.0
+
+
+def gather_around(x, axis, dim):
+    ways, here, turn = (lax.axis_size(axis), lax.axis_index(axis), x.shape[dim])
+    lengths = [n * ways if d == dim else n for d, n in enumerate(x.shape)]
+    full = lax.dynamic_update_slice_in_dim(jnp.zeros(lengths, x.dtype), x, here * turn, axis=dim)
+    going_up = going_down = x
+    for far in range(1, ways // 2 + 1):
+        going_up = lax.ppermute(going_up, axis, [(d, (d + 1) % ways) for d in range(ways)])
+        full = lax.dynamic_update_slice_in_dim(full, going_up, (here - far) % ways * turn, axis=dim)
+        if 2 * far < ways:
+            going_down = lax.ppermute(going_down, axis, [(d, (d - 1) % ways) for d in range(ways)])
+            full = lax.dynamic_update_slice_in_dim(
+                full, going_down, (here + far) % ways * turn, axis=dim
+            )
+    return full
 
 
 def bdot(form, left, right):
@@ -26,7 +42,7 @@
     scale = tokens ** (-0.5)
     full_mean, full_hess = (
         lax.all_gather(mean_state, "dp", axis=2, tiled=True),
-        lax.all_gather(hess_state, "dp", axis=2, tiled=True),
+        gather_around(hess_state, "dp", 2),
     )
     spread = jnp.sqrt(LAMBDA_SIZE * (full_hess + DELTA_DAMP))
     noise = noise_draw[0]

time: 321 us -> 340 us (1.059)
  starting transfers between devices: 40.3 us -> 61.9 us
  blocking collectives: 41.1 us -> 20.4 us
  waiting for transfers between devices: 172 us -> 191 us
    all_gather x1 -> x0, blocking collectives: 25.6 us -> none  [per_device(): lax.all_gather(hess_state, 'dp', axis=2, tiled=True)]
    ppermute x0 -> x15, starting transfers between devices: none -> 25.4 us  [the longest x7 18.6 us: gather_around(): lax.ppermute(going_down, axis, [(d, (d - 1) % ways) for d in range(ways)])]
    unnamed x2, waiting for transfers between devices: 113 us -> 132 us
    all_to_all x1, waiting for transfers between devices: 12.5 us -> 0.92 us  [per_device(): lax.all_to_all(back_left, 'mp', split_axis=1, concat_axis=2, tiled=True)]
    ppermute x0 -> x15, waiting for transfers between devices: none -> 8.91 us  [the longest x8 8.15 us: gather_around(): lax.ppermute(going_up, axis, [(d, (d + 1) % ways) for d in range(ways)])]
    all_to_all x1, waiting for transfers between devices: 1.99 us -> 10.1 us  [per_device(): lax.all_to_all(outer, 'mp', split_axis=1, concat_axis=2, tiled=True)]
    all_gather x1, blocking collectives: 15.5 us -> 20.4 us  [per_device(): lax.all_gather(mean_state, 'dp', axis=2, tiled=True)]
    all_to_all x1, starting transfers between devices: 5.07 us -> 9.8 us  [per_device(): lax.all_to_all(back_outer, 'mp', split_axis=1, concat_axis=2, tiled=True)]
  transfers between devices with their start and end apart: 7 -> 22, of which waited for: 7 -> 18; matrix products, arithmetic and copies ran while one was open for 9% -> 7% of each run, Pallas kernels for 0% -> 0%
where the time goes in v1:
time: 340 us; the launch traced here: 339 us
  waiting for transfers between devices  191 us (56%)
  starting transfers between devices  61.9 us (18%)
  local copies, waits for them, and re-layouts  29.2 us (9%)
  blocking collectives  20.4 us (6%)
  matrix products  18.2 us (5%)
  between operations  15.4 us (5%)
    unnamed x2, waiting for transfers between devices  132 us
    all_gather x1, blocking collectives, per_device(): lax.all_gather(mean_state, 'dp', axis=2, tiled=True)  20.4 us
    ppermute x7, starting transfers between devices, gather_around(): lax.ppermute(going_down, axis, [(d, (d - 1) % ways) for d in range(ways)])  18.6 us
    dot_general x15, matrix products, bdot(): return jnp.einsum(form, left, right, preferred_element_type=jnp.float32)  18.2 us
    all_to_all x1, waiting for transfers between devices, per_device(): lax.all_to_all(y_left, 'mp', split_axis=1, concat_axis=2, tiled=True)  11.1 us
    all_to_all x1, waiting for transfers between devices, per_device(): lax.all_to_all(back_outer, 'mp', split_axis=1, concat_axis=2, tiled=True)  10.8 us
    all_to_all x1, waiting for transfers between devices, per_device(): lax.all_to_all(outer, 'mp', split_axis=1, concat_axis=2, tiled=True)  10.1 us
    all_to_all x1, waiting for transfers between devices, per_device(): lax.all_to_all(back_right, 'mp', split_axis=1, concat_axis=2, tiled=True)  10 us
  transfers between devices with their start and end apart: 22, of which 18 were waited for; matrix products, arithmetic and copies ran while one was open for 7% of the time, Pallas kernels for 0%

profile of v1, /device:TPU:1, one launch (start us, length us, event | category | flops | bytes accessed | tf_op | source)
XLA Modules:
  0.0 338.8 jit_solution(17640364748662667432)
XLA Ops:
  7.2 3.5 %collective-permute-start = (f32[6,2,4,64]{3,2,1,0:T(4,128)}, f32[6,2,4,64]{3,2,1,0:T(4,128)S(1)}, u32[]{:S(2)}, u32[]{:S(2)}) collective-permute-start(f32[6,2,4,64]{3,2,1,0:T(4,128)} %param.9), channel_id=1, source_target_pairs={{0,32},{32,64},{64,96},{96,128},{128,160},{160,192},{192,224},{224... | collective-permute-start | bytes 36872 | tf_op jit(solution)/shard_map/ppermute | solution.py:19
  10.7 3.4 %collective-permute-start.1 = (f32[6,2,4,64]{3,2,1,0:T(4,128)}, f32[6,2,4,64]{3,2,1,0:T(4,128)S(1)}, u32[]{:S(2)}, u32[]{:S(2)}) collective-permute-start(f32[6,2,4,64]{3,2,1,0:T(4,128)} %param.9), channel_id=1, source_target_pairs={{0,480},{32,0},{64,32},{96,64},{128,96},{160,128},{192,160},{224,1... | collective-permute-start | bytes 36872 | tf_op jit(solution)/shard_map/ppermute | solution.py:22
  14.1 20.4 %all_gather.3 = f32[6,2,64,64]{3,1,0,2:T(2,128)S(1)} all-gather(f32[6,2,4,64]{3,1,0,2:T(2,128)S(1)} %copy.43), channel_id=1, replica_groups=mesh['dp'=16,'mp'=32] {'dp'}, dimensions={2}, use_global_device_ids=true | all-gather | bytes 208896 | tf_op jit(solution)/shard_map/all_gather | solution.py:44
  34.8 0.7 copy-done.6
  35.9 0.5 collective-permute-start.3
  36.4 0.7 collective-permute-done.2
  37.1 2.1 collective-permute-start.4
  39.2 1.4 collective-permute-start.5
  40.6 0.6 collective-permute-done.4
  41.2 1.2 collective-permute-start.6
  42.5 2.6 collective-permute-start.7
  45.0 0.6 collective-permute-done.6
  45.9 3.6 %collective-permute-start.9 = (f32[6,2,4,64]{3,2,1,0:T(4,128)S(1)}, f32[6,2,4,64]{3,2,1,0:T(4,128)S(1)}, u32[]{:S(2)}, u32[]{:S(2)}) collective-permute-start(f32[6,2,4,64]{3,2,1,0:T(4,128)S(1)} %collective-permute-done.7), channel_id=1, source_target_pairs={{0,480},{32,0},{64,32},{96,64},{128,96},{160,128},{192,160},{224,1... | collective-permute-start | bytes 36872 | tf_op jit(solution)/shard_map/ppermute | solution.py:22
  49.5 0.6 collective-permute-done.8
  50.3 3.6 %collective-permute-start.11 = (f32[6,2,4,64]{3,2,1,0:T(4,128)S(1)}, f32[6,2,4,64]{3,2,1,0:T(4,128)S(1)}, u32[]{:S(2)}, u32[]{:S(2)}) collective-permute-start(f32[6,2,4,64]{3,2,1,0:T(4,128)S(1)} %collective-permute-done.9), channel_id=1, source_target_pairs={{0,480},{32,0},{64,32},{96,64},{128,96},{160,128},{192,160},{224,1... | collective-permute-start | bytes 36872 | tf_op jit(solution)/shard_map/ppermute | solution.py:22
  54.0 0.6 collective-permute-done.10
  54.8 3.6 %collective-permute-start.13 = (f32[6,2,4,64]{3,2,1,0:T(4,128)S(1)}, f32[6,2,4,64]{3,2,1,0:T(4,128)S(1)}, u32[]{:S(2)}, u32[]{:S(2)}) collective-permute-start(f32[6,2,4,64]{3,2,1,0:T(4,128)S(1)} %collective-permute-done.11), channel_id=1, source_target_pairs={{0,480},{32,0},{64,32},{96,64},{128,96},{160,128},{192,160},{224,1... | collective-permute-start | bytes 36872 | tf_op jit(solution)/shard_map/ppermute | solution.py:22
  58.4 0.6 collective-permute-done.12
  59.3 4.3 %collective-permute-done.14 = f32[6,2,4,64]{3,2,1,0:T(4,128)S(1)} collective-permute-done((f32[6,2,4,64]{3,2,1,0:T(4,128)S(1)}, f32[6,2,4,64]{3,2,1,0:T(4,128)S(1)}, u32[]{:S(2)}, u32[]{:S(2)}) %collective-permute-start.14) | collective-permute-done | bytes 12320 | tf_op jit(solution)/shard_map/ppermute | solution.py:19
  64.0 1.4 copy.46
  65.4 9.8 %all-to-all-start = ((bf16[2048,64,2]{0,2,1:T(2,128)(2,1)}), bf16[2048,64,2]{0,2,1:T(2,128)(2,1)S(1)}, u32[]{:S(2)}, u32[]{:S(2)}) async-start(bf16[2048,64,2]{0,2,1:T(2,128)(2,1)} %copy.46), calls=%async_computation | async-start | bytes 1048576 | tf_op jit(solution)/shard_map/all_to_all | solution.py:70
  75.8 1.3 copy.54
  77.1 10.8 %all-to-all-done = bf16[2048,64,2]{0,2,1:T(2,128)(2,1)S(1)} async-done(((bf16[2048,64,2]{0,2,1:T(2,128)(2,1)}), bf16[2048,64,2]{0,2,1:T(2,128)(2,1)S(1)}, u32[]{:S(2)}, u32[]{:S(2)}) %all-to-all-start) | async-done | bytes 524320 | tf_op jit(solution)/shard_map/all_to_all | solution.py:70
  88.0 6.1 %all-to-all-start.2 = ((bf16[2048,64,2]{0,2,1:T(2,128)(2,1)}), bf16[2048,64,2]{0,2,1:T(2,128)(2,1)S(1)}, u32[]{:S(2)}, u32[]{:S(2)}) async-start(bf16[2048,64,2]{0,2,1:T(2,128)(2,1)} %copy.54), calls=%async_computation.2 | async-start | bytes 1048576 | tf_op jit(solution)/shard_map/all_to_all | solution.py:54
  94.1 0.3 fusion.1
  94.5 1.3 copy.50
  95.8 11.1 %all-to-all-done.2 = bf16[2048,64,2]{0,2,1:T(2,128)(2,1)S(1)} async-done(((bf16[2048,64,2]{0,2,1:T(2,128)(2,1)}), bf16[2048,64,2]{0,2,1:T(2,128)(2,1)S(1)}, u32[]{:S(2)}, u32[]{:S(2)}) %all-to-all-start.2) | async-done | bytes 524320 | tf_op jit(solution)/shard_map/all_to_all | solution.py:54
  106.9 5.9 %all-to-all-start.1 = ((bf16[2048,64,2]{0,2,1:T(2,128)(2,1)}), bf16[2048,64,2]{0,2,1:T(2,128)(2,1)S(1)}, u32[]{:S(2)}, u32[]{:S(2)}) async-start(bf16[2048,64,2]{0,2,1:T(2,128)(2,1)} %copy.50), calls=%async_computation.1 | async-start | bytes 1048576 | tf_op jit(solution)/shard_map/all_to_all | solution.py:55
  112.8 0.4 copy.87
  113.4 0.4 copy.85
  113.9 2.0 convolution_bitcast_fusion.2
  116.0 2.1 convolution_bitcast_fusion
  118.1 7.6 %all-to-all-done.1 = bf16[2048,64,2]{0,2,1:T(2,128)(2,1)S(1)} async-done(((bf16[2048,64,2]{0,2,1:T(2,128)(2,1)}), bf16[2048,64,2]{0,2,1:T(2,128)(2,1)S(1)}, u32[]{:S(2)}, u32[]{:S(2)}) %all-to-all-start.1) | async-done | bytes 524320 | tf_op jit(solution)/shard_map/all_to_all | solution.py:55
  125.6 0.4 copy.86
  126.2 3.2 multiply_convert_fusion
  129.4 1.1 fusion.5
  130.5 1.3 copy.62
  131.9 5.2 %all-to-all-start.5 = ((bf16[2048,64,2]{0,2,1:T(2,128)(2,1)}), bf16[2048,64,2]{0,2,1:T(2,128)(2,1)}, u32[]{:S(2)}, u32[]{:S(2)}) async-start(bf16[2048,64,2]{0,2,1:T(2,128)(2,1)} %copy.62), calls=%async_computation.5 | async-start | bytes 1048576 | tf_op jit(solution)/shard_map/all_to_all | solution.py:68
  137.0 1.3 fusion.4
  138.4 1.4 copy.59
  139.8 10.1 %all-to-all-done.5 = bf16[2048,64,2]{0,2,1:T(2,128)(2,1)} async-done(((bf16[2048,64,2]{0,2,1:T(2,128)(2,1)}), bf16[2048,64,2]{0,2,1:T(2,128)(2,1)}, u32[]{:S(2)}, u32[]{:S(2)}) %all-to-all-start.5) | async-done | bytes 524320 | tf_op jit(solution)/shard_map/all_to_all | solution.py:68
  149.9 4.8 %all-to-all-start.4 = ((bf16[2048,64,2]{0,2,1:T(2,128)(2,1)}), bf16[2048,64,2]{0,2,1:T(2,128)(2,1)}, u32[]{:S(2)}, u32[]{:S(2)}) async-start(bf16[2048,64,2]{0,2,1:T(2,128)(2,1)} %copy.59), calls=%async_computation.4 | async-start | bytes 1048576 | tf_op jit(solution)/shard_map/all_to_all | solution.py:82
  154.7 1.3 fusion.3
  156.0 1.3 copy.57
  157.4 10.0 %all-to-all-done.4 = bf16[2048,64,2]{0,2,1:T(2,128)(2,1)} async-done(((bf16[2048,64,2]{0,2,1:T(2,128)(2,1)}), bf16[2048,64,2]{0,2,1:T(2,128)(2,1)}, u32[]{:S(2)}, u32[]{:S(2)}) %all-to-all-start.4) | async-done | bytes 524320 | tf_op jit(solution)/shard_map/all_to_all | solution.py:82
  167.4 4.6 %all-to-all-start.3 = ((bf16[2048,64,2]{0,2,1:T(2,128)(2,1)}), bf16[2048,64,2]{0,2,1:T(2,128)(2,1)}, u32[]{:S(2)}, u32[]{:S(2)}) async-start(bf16[2048,64,2]{0,2,1:T(2,128)(2,1)} %copy.57), calls=%async_computation.3 | async-start | bytes 1048576 | tf_op jit(solution)/shard_map/all_to_all | solution.py:81
  172.1 2.2 copy.82
  174.3 2.0 all_to_all.101
  176.3 2.2 copy.83
  178.5 2.0 all_to_all.97
  180.5 2.0 fusion.12
  182.5 1.5 copy.65
  184.0 0.9 all-to-all-done.3
  185.0 2.2 copy.84
  187.2 2.1 all_to_all.93
  189.2 2.0 fusion.15
  191.2 0.9 copy.64
  192.1 1.4 fusion.14
  194.2 0.7 copy-done.1
  195.2 0.8 copy-done.2
  196.0 0.9 fusion.19
  196.9 1.3 dynamic-slice
  198.8 131.6 %all-reduce.5.cloned.1.call-done = (f32[6,2,64,64]{3,2,1,0:T(8,128)}, f32[6,2,64,64]{3,2,1,0:T(8,128)}) async-done(((f32[6,2,64,64]{3,2,1,0:T(8,128)}, f32[6,2,64,64]{3,2,1,0:T(8,128)}), (f32[6,2,64,64]{3,2,1,0:T(8,128)}, f32[6,2,64,64]{3,2,1,0:T(8,128)})) %all-reduce.5.cloned.1.call-update) | async-done | bytes 393232
  330.4 1.5 divide_subtract_fusion
  (71 shorter events, 3.8 us)
Async XLA Ops:
  7.2 6.9 %copy-start.9 = (f32[6,2,4,64]{3,2,1,0:T(4,128)S(1)}, f32[6,2,4,64]{3,2,1,0:T(4,128)}, u32[]{:S(2)}) copy-start(f32[6,2,4,64]{3,2,1,0:T(4,128)} %param.8) | copy-start | bytes 36868
  7.2 28.7 %collective-permute-start = (f32[6,2,4,64]{3,2,1,0:T(4,128)}, f32[6,2,4,64]{3,2,1,0:T(4,128)S(1)}, u32[]{:S(2)}, u32[]{:S(2)}) collective-permute-start(f32[6,2,4,64]{3,2,1,0:T(4,128)} %param.9), channel_id=1, source_target_pairs={{0,32},{32,64},{64,96},{96,128},{128,160},{160,192},{192,224},{224... | collective-permute-start | bytes 36872 | tf_op jit(solution)/shard_map/ppermute | solution.py:19
  10.7 25.3 %collective-permute-start.1 = (f32[6,2,4,64]{3,2,1,0:T(4,128)}, f32[6,2,4,64]{3,2,1,0:T(4,128)S(1)}, u32[]{:S(2)}, u32[]{:S(2)}) collective-permute-start(f32[6,2,4,64]{3,2,1,0:T(4,128)} %param.9), channel_id=1, source_target_pairs={{0,480},{32,0},{64,32},{96,64},{128,96},{160,128},{192,160},{224,1... | collective-permute-start | bytes 36872 | tf_op jit(solution)/shard_map/ppermute | solution.py:22
  14.1 20.5 %copy-start.11 = (f32[6,2,4,64]{3,2,1,0:T(4,128)S(1)}, f32[6,2,4,64]{3,2,1,0:T(4,128)}, u32[]{:S(2)}) copy-start(f32[6,2,4,64]{3,2,1,0:T(4,128)} %param.9) | copy-start | bytes 36868
  34.5 1.0 copy-start.6
  35.8 27.8 %copy-start.3 = (f32[1,6,2,64,64]{4,3,2,1,0:T(8,128)S(1)}, f32[1,6,2,64,64]{4,3,2,1,0:T(8,128)}, u32[]{:S(2)}) copy-start(f32[1,6,2,64,64]{4,3,2,1,0:T(8,128)} %param.11) | copy-start | bytes 589828
  35.9 1.2 collective-permute-start.2
  35.9 3.3 collective-permute-start.3
  37.1 4.1 %collective-permute-start.4 = (f32[6,2,4,64]{3,2,1,0:T(4,128)S(1)}, f32[6,2,4,64]{3,2,1,0:T(4,128)S(1)}, u32[]{:S(2)}, u32[]{:S(2)}) collective-permute-start(f32[6,2,4,64]{3,2,1,0:T(4,128)S(1)} %collective-permute-done.2), channel_id=1, source_target_pairs={{0,32},{32,64},{64,96},{96,128},{128,160},{160,192},{192,224},{224... | collective-permute-start | bytes 36872 | tf_op jit(solution)/shard_map/ppermute | solution.py:19
  39.2 3.3 collective-permute-start.5
  41.2 4.5 %collective-permute-start.6 = (f32[6,2,4,64]{3,2,1,0:T(4,128)S(1)}, f32[6,2,4,64]{3,2,1,0:T(4,128)S(1)}, u32[]{:S(2)}, u32[]{:S(2)}) collective-permute-start(f32[6,2,4,64]{3,2,1,0:T(4,128)S(1)} %collective-permute-done.4), channel_id=1, source_target_pairs={{0,32},{32,64},{64,96},{96,128},{128,160},{160,192},{192,224},{224... | collective-permute-start | bytes 36872 | tf_op jit(solution)/shard_map/ppermute | solution.py:19
  42.5 3.4 %collective-permute-start.7 = (f32[6,2,4,64]{3,2,1,0:T(4,128)S(1)}, f32[6,2,4,64]{3,2,1,0:T(4,128)S(1)}, u32[]{:S(2)}, u32[]{:S(2)}) collective-permute-start(f32[6,2,4,64]{3,2,1,0:T(4,128)S(1)} %collective-permute-done.5), channel_id=1, source_target_pairs={{0,480},{32,0},{64,32},{96,64},{128,96},{160,128},{192,160},{224,1... | collective-permute-start | bytes 36872 | tf_op jit(solution)/shard_map/ppermute | solution.py:22
  45.7 4.5 %collective-permute-start.8 = (f32[6,2,4,64]{3,2,1,0:T(4,128)S(1)}, f32[6,2,4,64]{3,2,1,0:T(4,128)S(1)}, u32[]{:S(2)}, u32[]{:S(2)}) collective-permute-start(f32[6,2,4,64]{3,2,1,0:T(4,128)S(1)} %collective-permute-done.6), channel_id=1, source_target_pairs={{0,32},{32,64},{64,96},{96,128},{128,160},{160,192},{192,224},{224... | collective-permute-start | bytes 36872 | tf_op jit(solution)/shard_map/ppermute | solution.py:19
  45.9 4.5 %collective-permute-start.9 = (f32[6,2,4,64]{3,2,1,0:T(4,128)S(1)}, f32[6,2,4,64]{3,2,1,0:T(4,128)S(1)}, u32[]{:S(2)}, u32[]{:S(2)}) collective-permute-start(f32[6,2,4,64]{3,2,1,0:T(4,128)S(1)} %collective-permute-done.7), channel_id=1, source_target_pairs={{0,480},{32,0},{64,32},{96,64},{128,96},{160,128},{192,160},{224,1... | collective-permute-start | bytes 36872 | tf_op jit(solution)/shard_map/ppermute | solution.py:22
  50.2 4.5 %collective-permute-start.10 = (f32[6,2,4,64]{3,2,1,0:T(4,128)S(1)}, f32[6,2,4,64]{3,2,1,0:T(4,128)S(1)}, u32[]{:S(2)}, u32[]{:S(2)}) collective-permute-start(f32[6,2,4,64]{3,2,1,0:T(4,128)S(1)} %collective-permute-done.8), channel_id=1, source_target_pairs={{0,32},{32,64},{64,96},{96,128},{128,160},{160,192},{192,224},{224... | collective-permute-start | bytes 36872 | tf_op jit(solution)/shard_map/ppermute | solution.py:19
  50.3 4.5 %collective-permute-start.11 = (f32[6,2,4,64]{3,2,1,0:T(4,128)S(1)}, f32[6,2,4,64]{3,2,1,0:T(4,128)S(1)}, u32[]{:S(2)}, u32[]{:S(2)}) collective-permute-start(f32[6,2,4,64]{3,2,1,0:T(4,128)S(1)} %collective-permute-done.9), channel_id=1, source_target_pairs={{0,480},{32,0},{64,32},{96,64},{128,96},{160,128},{192,160},{224,1... | collective-permute-start | bytes 36872 | tf_op jit(solution)/shard_map/ppermute | solution.py:22
  54.6 4.5 %collective-permute-start.12 = (f32[6,2,4,64]{3,2,1,0:T(4,128)S(1)}, f32[6,2,4,64]{3,2,1,0:T(4,128)S(1)}, u32[]{:S(2)}, u32[]{:S(2)}) collective-permute-start(f32[6,2,4,64]{3,2,1,0:T(4,128)S(1)} %collective-permute-done.10), channel_id=1, source_target_pairs={{0,32},{32,64},{64,96},{96,128},{128,160},{160,192},{192,224},{224... | collective-permute-start | bytes 36872 | tf_op jit(solution)/shard_map/ppermute | solution.py:19
  54.8 4.5 %collective-permute-start.13 = (f32[6,2,4,64]{3,2,1,0:T(4,128)S(1)}, f32[6,2,4,64]{3,2,1,0:T(4,128)S(1)}, u32[]{:S(2)}, u32[]{:S(2)}) collective-permute-start(f32[6,2,4,64]{3,2,1,0:T(4,128)S(1)} %collective-permute-done.11), channel_id=1, source_target_pairs={{0,480},{32,0},{64,32},{96,64},{128,96},{160,128},{192,160},{224,1... | collective-permute-start | bytes 36872 | tf_op jit(solution)/shard_map/ppermute | solution.py:22
  59.1 4.5 %collective-permute-start.14 = (f32[6,2,4,64]{3,2,1,0:T(4,128)S(1)}, f32[6,2,4,64]{3,2,1,0:T(4,128)S(1)}, u32[]{:S(2)}, u32[]{:S(2)}) collective-permute-start(f32[6,2,4,64]{3,2,1,0:T(4,128)S(1)} %collective-permute-done.12), channel_id=1, source_target_pairs={{0,32},{32,64},{64,96},{96,128},{128,160},{160,192},{192,224},{224... | collective-permute-start | bytes 36872 | tf_op jit(solution)/shard_map/ppermute | solution.py:19
  63.7 30.4 %copy-start.5 = (bf16[6,2,64,64]{3,2,1,0:T(8,128)(2,1)}, bf16[6,2,64,64]{3,2,1,0:T(8,128)(2,1)S(1)}, u32[]{:S(2)}) copy-start(bf16[6,2,64,64]{3,2,1,0:T(8,128)(2,1)S(1)} %fusion.18) | copy-start | bytes 294916
  65.4 9.8 %copy-start.7 = (bf16[2048,128]{1,0:T(8,128)(2,1)S(1)}, bf16[2048,128]{1,0:T(8,128)(2,1)}, u32[]{:S(2)}) copy-start(bf16[2048,128]{1,0:T(8,128)(2,1)} %param.6) | copy-start | bytes 1572868
  65.4 22.6 %all-to-all-start = ((bf16[2048,64,2]{0,2,1:T(2,128)(2,1)}), bf16[2048,64,2]{0,2,1:T(2,128)(2,1)S(1)}, u32[]{:S(2)}, u32[]{:S(2)}) async-start(bf16[2048,64,2]{0,2,1:T(2,128)(2,1)} %copy.46), calls=%async_computation | async-start | bytes 1048576 | tf_op jit(solution)/shard_map/all_to_all | solution.py:70
  88.0 18.9 %all-to-all-start.2 = ((bf16[2048,64,2]{0,2,1:T(2,128)(2,1)}), bf16[2048,64,2]{0,2,1:T(2,128)(2,1)S(1)}, u32[]{:S(2)}, u32[]{:S(2)}) async-start(bf16[2048,64,2]{0,2,1:T(2,128)(2,1)} %copy.54), calls=%async_computation.2 | async-start | bytes 1048576 | tf_op jit(solution)/shard_map/all_to_all | solution.py:54
  106.9 18.7 %all-to-all-start.1 = ((bf16[2048,64,2]{0,2,1:T(2,128)(2,1)}), bf16[2048,64,2]{0,2,1:T(2,128)(2,1)S(1)}, u32[]{:S(2)}, u32[]{:S(2)}) async-start(bf16[2048,64,2]{0,2,1:T(2,128)(2,1)} %copy.50), calls=%async_computation.1 | async-start | bytes 1048576 | tf_op jit(solution)/shard_map/all_to_all | solution.py:55
  131.9 18.0 %all-to-all-start.5 = ((bf16[2048,64,2]{0,2,1:T(2,128)(2,1)}), bf16[2048,64,2]{0,2,1:T(2,128)(2,1)}, u32[]{:S(2)}, u32[]{:S(2)}) async-start(bf16[2048,64,2]{0,2,1:T(2,128)(2,1)} %copy.62), calls=%async_computation.5 | async-start | bytes 1048576 | tf_op jit(solution)/shard_map/all_to_all | solution.py:68
  149.9 17.6 %all-to-all-start.4 = ((bf16[2048,64,2]{0,2,1:T(2,128)(2,1)}), bf16[2048,64,2]{0,2,1:T(2,128)(2,1)}, u32[]{:S(2)}, u32[]{:S(2)}) async-start(bf16[2048,64,2]{0,2,1:T(2,128)(2,1)} %copy.59), calls=%async_computation.4 | async-start | bytes 1048576 | tf_op jit(solution)/shard_map/all_to_all | solution.py:82
  167.4 17.6 %all-to-all-start.3 = ((bf16[2048,64,2]{0,2,1:T(2,128)(2,1)}), bf16[2048,64,2]{0,2,1:T(2,128)(2,1)}, u32[]{:S(2)}, u32[]{:S(2)}) async-start(bf16[2048,64,2]{0,2,1:T(2,128)(2,1)} %copy.57), calls=%async_computation.3 | async-start | bytes 1048576 | tf_op jit(solution)/shard_map/all_to_all | solution.py:81
  172.0 158.4 %all-reduce.5.cloned.1.call-start = ((), (), s32[]{:S(2)}) async-start(), calls=%async_computation.6 | async-start | bytes 1572864
  192.1 1.4 copy-start.8
  192.1 1.4 copy-start
  193.9 1.0 copy-start.1
  194.9 1.1 copy-start.4
  195.2 0.8 copy-start.2
  196.9 133.6 %copy-start.12 = (f32[6,2,4,64]{3,2,1,0:T(4,128)S(1)}, f32[6,2,4,64]{3,2,1,0:T(4,128)}, u32[]{:S(2)}) copy-start(f32[6,2,4,64]{3,2,1,0:T(4,128)} %param.9) | copy-start | bytes 36868
  196.9 133.6 %copy-start.13 = (f32[6,2,4,64]{3,2,1,0:T(4,128)S(1)}, f32[6,2,4,64]{3,2,1,0:T(4,128)}, u32[]{:S(2)}) copy-start(f32[6,2,4,64]{3,2,1,0:T(4,128)} %param.10) | copy-start | bytes 36868
  196.9 133.6 %copy-start.10 = (f32[6,2,4,64]{3,2,1,0:T(4,128)S(1)}, f32[6,2,4,64]{3,2,1,0:T(4,128)}, u32[]{:S(2)}) copy-start(f32[6,2,4,64]{3,2,1,0:T(4,128)} %param.8) | copy-start | bytes 36868
Sparse Core Ops, SparseCore 0:
  197.0 133.3 all-reduce.4
